TPU v7x, 128 devices: a whole 4x4x4 slice. The times are simulated.
128 devices in a mesh: blk: 8 (over x_lo, y), grid: 16 (over x_hi, z, core).
Axes of the slice: x: 4 (x_hi: 2, x_lo: 2; x = x_hi * 2 + x_lo), y: 4, z: 4, core: 2. Of those that a mesh axis runs over, the one named last changes fastest.
Arguments:
- conn: int32 [2048, 9], P(('blk', 'grid')), may hold values from 0 to 2047, as said below
- extract: float32 [9, 9, 2048], P(None, None, ('blk', 'grid')), may hold values from 0.1 to 1
- points: float32 [3, 9, 2048], P(None, None, ('blk', 'grid')), as said below
Outputs:
- factor: float32 [1, 2048, 2, 1024], P(None, 'grid', None, 'blk')
Inputs may be any that keep to these rules, and one draw needn't show every extreme that they name: `conn`: element e = ix 32 + iy of the periodic 64 x 32 grid of elements names the functions ((ix + s) mod 64) * 32 + (iy + t) mod 32 for s, t in 0, 1, 2, each once, in an order that differs from element to element. The 9 points of element e = ix 32 + iy are the 3 x 3 Gauss points of the cell [ix / 64, (ix + 1) / 64] x [iy / 64, (iy + 1) / 64], each coordinate then moved by at most 3.5 / 64; points[2] is positive.
All inputs are finite; a program needn't handle non-finite values.
Results may differ from a plain program's by a relative error of at most 0.0003.
Values sent between devices are 32-bit elements; how exact they have to be, the bound alone decides.
A program may use at most 128 MiB of HBM per device.

v0:
```python
import math
import jax
import jax.numpy as jnp
from jax import lax
from jax.sharding import PartitionSpec as P

M = 2048
EX = 64
EY = 32
QP = 9
TB = 128
kernel_gain = 0.02
mass_shift = 0.05


def spread(array, axis, root):
    mine = lax.axis_index(axis) == root
    return lax.psum(jnp.where(mine, array, jnp.zeros_like(array)), axis)


def bernstein_table():
    spread_root = 0.5 * math.sqrt(0.6)
    gauss_nodes = [0.5 - spread_root, 0.5, 0.5 + spread_root]

    def bern_poly(which, where):
        return [(1.0 - where) ** 2, 2.0 * where * (1.0 - where), where * where][which]

    table_rows = []
    for i in range(3):
        for j in range(3):
            table_row = []
            for a in range(3):
                for b in range(3):
                    table_row.append(bern_poly(a, gauss_nodes[i]) * bern_poly(b, gauss_nodes[j]))
            table_rows.append(table_row)
    return jnp.asarray(table_rows, jnp.float32)


def torus_square(first_x, first_y, second_x, second_y):
    height = EY / EX
    gap_x = jnp.abs(first_x - second_x)
    gap_x = jnp.minimum(gap_x, jnp.abs(1.0 - gap_x))
    gap_y = jnp.abs(first_y - second_y)
    gap_y = jnp.minimum(gap_y, jnp.abs(height - gap_y))
    return gap_x * gap_x + gap_y * gap_y


def kernel_rows(test_x, test_y, trial_x, trial_y, trial_w):
    distance = torus_square(test_x[:, None], test_y[:, None], trial_x[None, :], trial_y[None, :])
    return kernel_gain * trial_w[None, :] * (1.0 + distance * (EX * EX / 4.0)) ** (-1.75)


def local_values(extract_cube):
    return jnp.einsum(
        "kb,abn->nka", bernstein_table(), extract_cube, precision=lax.Precision.HIGHEST
    )


def basis_rows(values, links):
    count = links.shape[0]
    slot = jnp.arange(count * QP, dtype=jnp.int32).reshape(count, QP)
    row_index = jnp.broadcast_to(slot[:, :, None], (count, QP, QP))
    col_index = jnp.broadcast_to(links[:, None, :], (count, QP, QP))
    return jnp.zeros((count * QP, M), jnp.float32).at[row_index, col_index].add(values)


def window_width():
    wide = 128 + 4 * EY
    return wide


def fold_window(potential_wide):
    extra = potential_wide.shape[1] - M
    return potential_wide[:, :M] + jnp.pad(potential_wide[:, M:], ((0, 0), (0, M - extra)))


def tile_target(links, grid_size, tile_rows):
    tile = links // TB
    return tile % grid_size * (tile_rows * TB) + tile // grid_size * TB + links % TB


def add_potential(state, piece, first_element, test_x, test_y):
    points_flat, extract_flat, links_flat = piece
    count = points_flat.shape[1]
    span = math.gcd(count, 128)
    width = window_width()
    window_iota = jnp.arange(width, dtype=jnp.int32)

    def step(index, inner):
        potential_wide, total = inner
        first = index * span
        part_points = lax.dynamic_slice_in_dim(points_flat, first, span, 1).reshape(3, QP, span)
        part_extract = lax.dynamic_slice_in_dim(extract_flat, first, span, 1).reshape(QP, QP, span)
        part_links = lax.dynamic_slice_in_dim(links_flat, first, span, 1).T
        kernel_block = kernel_rows(
            test_x,
            test_y,
            part_points[0].T.reshape(-1),
            part_points[1].T.reshape(-1),
            part_points[2].T.reshape(-1),
        )
        total = total + jnp.sum(kernel_block, axis=1)
        offset = (first_element + first) // EY * EY
        local = (part_links - offset) % M
        ones = (local[:, :, None] == window_iota[None, None, :]).astype(jnp.float32)
        trial_phi = jnp.einsum(
            "eka,eaw->ekw", local_values(part_extract), ones, precision=lax.Precision.HIGHEST
        ).reshape(span * QP, width)
        block = jnp.dot(
            kernel_block,
            trial_phi,
            precision=lax.Precision.HIGHEST,
            preferred_element_type=jnp.float32,
        )
        current = lax.dynamic_slice_in_dim(potential_wide, offset, width, 1)
        potential_wide = lax.dynamic_update_slice_in_dim(potential_wide, current + block, offset, 1)
        return (potential_wide, total)

    return lax.fori_loop(0, count // span, step, state)


def shards(conn, extract, points):
    count = conn.shape[0]
    rows = count * QP
    links_flat = conn.T
    extract_flat = extract.reshape(QP * QP, count)
    points_flat = points.reshape(3 * QP, count)
    own_x = points[0].T.reshape(-1)
    own_y = points[1].T.reshape(-1)
    own_w = points[2].T.reshape(-1)
    own_values = local_values(extract)
    test_phi = basis_rows(own_values, conn)
    width = window_width()
    start_state = (jnp.zeros((rows, M + width), jnp.float32), jnp.zeros((rows,), jnp.float32))
    grid_size = lax.axis_size("grid")
    blk_size = lax.axis_size("blk")
    grid_at = lax.axis_index("grid")
    blk_at = lax.axis_index("blk")
    tile_rows = M // (TB * grid_size)
    tile_cols = M // (TB * blk_size)
    band = tile_cols * TB
    potential_wide, total = add_potential(
        start_state,
        (
            lax.all_gather(points_flat, ("blk", "grid"), axis=1, tiled=True),
            lax.all_gather(extract_flat, ("blk", "grid"), axis=1, tiled=True),
            lax.all_gather(links_flat, ("blk", "grid"), axis=1, tiled=True),
        ),
        jnp.int32(0),
        own_x,
        own_y,
    )
    potential = fold_window(potential_wide)
    share = own_w[:, None] * ((mass_shift + total)[:, None] * test_phi - potential)
    own_contrib = jnp.einsum(
        "eka,ekm->eam", own_values, share.reshape(count, QP, M), precision=lax.Precision.HIGHEST
    )
    split_cols = (
        own_contrib.reshape(rows, tile_cols, blk_size, TB)
        .transpose(2, 0, 1, 3)
        .reshape(blk_size, rows, band)
    )
    targets = tile_target(conn.reshape(-1), grid_size, tile_rows)
    placed = (
        jnp.zeros((blk_size, grid_size * tile_rows * TB, band), jnp.float32)
        .at[:, targets]
        .add(split_cols)
    )
    term = placed.reshape(blk_size * grid_size, -1)
    stiff = lax.psum_scatter(term, ("blk", "grid"), scatter_dimension=0, tiled=True).reshape(
        tile_rows, TB, tile_cols, TB
    )
    column_tiles = stiff[:, :, 0, :]
    mine = spread(column_tiles, "blk", 0)
    panel_tiles = lax.all_gather(mine, "grid", axis=0, tiled=True)
    panel = panel_tiles.reshape(grid_size, tile_rows, TB, TB).transpose(1, 0, 2, 3).reshape(M, TB)
    head = panel[:TB]
    lower = jnp.linalg.cholesky(0.5 * (head + head.T))
    rest = lax.linalg.triangular_solve(
        lower, panel[TB:], left_side=False, lower=True, transpose_a=True
    )
    factor_cols = jnp.concatenate([lower, rest], axis=0)
    row_part = lax.dynamic_index_in_dim(
        factor_cols.reshape(tile_rows, grid_size, TB, TB), grid_at, 1, keepdims=False
    )
    col_part = lax.dynamic_index_in_dim(
        factor_cols.reshape(tile_cols, blk_size, TB, TB), blk_at, 1, keepdims=False
    )
    update = jnp.einsum("xuw,yvw->xuyv", row_part, col_part, precision=lax.Precision.HIGHEST)
    tile_row = (jnp.arange(tile_rows, dtype=jnp.int32) * grid_size + grid_at)[:, None, None, None]
    tile_col = (jnp.arange(tile_cols, dtype=jnp.int32) * blk_size + blk_at)[None, None, :, None]
    whole_row = tile_row * TB + jnp.arange(TB, dtype=jnp.int32)[None, :, None, None]
    whole_col = tile_col * TB + jnp.arange(TB, dtype=jnp.int32)[None, None, None, :]
    trailing = stiff - update
    result = jnp.where(
        tile_col == 0, row_part[:, :, None, :], jnp.where(tile_row == 0, 0.0, trailing)
    )
    return jnp.where(whole_row >= whole_col, result, 0.0)


def solution(mesh):
    in_specs = (
        P(("blk", "grid"), None),
        P(None, None, ("blk", "grid")),
        P(None, None, ("blk", "grid")),
    )
    out_specs = P(None, "grid", None, "blk")
    return jax.shard_map(shards, mesh=mesh, in_specs=in_specs, out_specs=out_specs, check_vma=False)
```

profile of v0, /device:TPU:1, one launch (start us, length us, event | category | flops | bytes accessed | tf_op | source)
XLA Modules:
  0.0 1185.3 jit_solution(11756267952525601225)
XLA Ops:
  13.7 182.9 %all_gather.13 = f32[81,2048]{0,1:T(8,128)S(1)} all-gather(f32[81,16]{0,1:T(8,128)S(1)} %copy.82), channel_id=1, replica_groups=mesh['blk'=8,'grid'=16] {'blk','grid'}, dimensions={1}, use_global_device_ids=true | all-gather | bytes 668736 | tf_op jit(solution)/shard_map/all_gather | solution.py:146
  197.9 183.5 %all_gather.12 = f32[27,2048]{0,1:T(8,128)} all-gather(f32[27,16]{0,1:T(8,128)S(1)} %reshape.418), channel_id=1, replica_groups=mesh['blk'=8,'grid'=16] {'blk','grid'}, dimensions={1}, use_global_device_ids=true | all-gather | bytes 222912 | tf_op jit(solution)/shard_map/all_gather | solution.py:145
  381.4 184.8 %all_gather.14 = s32[9,2048]{0,1:T(8,128)} all-gather(s32[9,16]{0,1:T(8,128)S(1)} %bitcast.107), channel_id=1, replica_groups=mesh['blk'=8,'grid'=16] {'blk','grid'}, dimensions={1}, use_global_device_ids=true | all-gather | bytes 74304 | tf_op jit(solution)/shard_map/all_gather | solution.py:147
  568.2 172.8 %while.20 = (s32[]{:T(128)}, f32[144,2304]{1,0:T(8,128)}, f32[144]{0:T(256)S(1)}, f32[27,2048]{0,1:T(8,128)}, f32[16,9]{1,0:T(8,128)}, /*index=5*/f32[16,9]{1,0:...) while((s32[]{:T(128)}, f32[144,2304]{1,0:T(8,128)}, ...), condition=%wide.wide.region_2.3_spmd.clone.clone, body=%wide.wide.region_0.2_spmd.sunk.clone.clone.sunk | while | flops 548399360 | bytes 5783860 | solution.py:119
  570.6 1.5 fusion.61
  574.0 2.4 convolution_add_fusion.3
  576.4 1.7 dynamic_update_slice.15
  581.4 1.5 fusion.61
  584.8 2.4 convolution_add_fusion.3
  587.2 1.7 dynamic_update_slice.15
  592.3 1.5 fusion.61
  595.7 2.4 convolution_add_fusion.3
  598.1 1.7 dynamic_update_slice.15
  603.1 1.5 fusion.61
  606.5 2.4 convolution_add_fusion.3
  608.9 1.7 dynamic_update_slice.15
  613.9 1.5 fusion.61
  617.3 2.4 convolution_add_fusion.3
  619.7 1.7 dynamic_update_slice.15
  624.6 1.5 fusion.61
  628.0 2.4 convolution_add_fusion.3
  630.4 1.7 dynamic_update_slice.15
  638.8 2.4 convolution_add_fusion.3
  641.2 1.7 dynamic_update_slice.15
  646.2 1.5 fusion.61
  649.6 2.4 convolution_add_fusion.3
  652.0 1.7 dynamic_update_slice.15
  657.1 1.5 fusion.61
  660.5 2.4 convolution_add_fusion.3
  662.9 1.7 dynamic_update_slice.15
  667.9 1.5 fusion.61
  671.3 2.4 convolution_add_fusion.3
  673.7 1.7 dynamic_update_slice.15
  678.7 1.5 fusion.61
  682.1 2.4 convolution_add_fusion.3
  684.5 1.7 dynamic_update_slice.15
  689.5 1.5 fusion.61
  692.9 2.4 convolution_add_fusion.3
  695.3 1.7 dynamic_update_slice.15
  700.3 1.5 fusion.61
  703.7 2.4 convolution_add_fusion.3
  706.1 1.7 dynamic_update_slice.15
  711.1 1.5 fusion.61
  714.5 2.4 convolution_add_fusion.3
  716.9 1.7 dynamic_update_slice.15
  721.9 1.5 fusion.61
  725.3 2.4 convolution_add_fusion.3
  727.7 1.7 dynamic_update_slice.15
  732.7 1.5 fusion.61
  736.1 2.4 convolution_add_fusion.3
  738.5 1.7 dynamic_update_slice.15
  745.1 10.7 scatter_custom_fusion.1
  757.6 1.5 subtract_multiply_fusion
  759.3 3.3 fusion.33
  762.6 1.6 reshape.384
  764.3 6.0 broadcast_in_dim.83
  770.3 16.2 %scatter_fusion = f32[8,2048,256]{2,0,1:T(8,128)} fusion(f32[8,2048,256]{2,0,1:T(8,128)} %broadcast_in_dim.83, s32[144]{0:T(256)S(1)} %bitcast.113, f32[144,8,256]{2,1,0:T(8,128)S(1)} %bitcast.99), kind=kCustom, calls=%fused_computation | custom fusion | flops 294912 | bytes 3539520 | tf_op jit(solution)/shard_map/scatter-add | solution.py:167
  786.4 15.8 %copy.93 = f32[8,2048,256]{2,1,0:T(8,128)} copy(f32[8,2048,256]{2,0,1:T(8,128)} %scatter_fusion) | data formatting | bytes 33554432 | tf_op jit(solution)/shard_map/scatter-add | solution.py:167
  802.3 18.2 %reshape.386 = f32[128,32768]{1,0:T(8,128)} reshape(f32[8,2048,256]{2,1,0:T(8,128)} %copy.93) | data formatting | bytes 33554432 | tf_op jit(solution)/shard_map/reshape | solution.py:169
  820.6 210.2 %all-reduce.7.cloned.1.call-done = f32[128,32768]{1,0:T(8,128)} async-done(((f32[128,32768]{1,0:T(8,128)}), f32[128,32768]{1,0:T(8,128)}) %all-reduce.7.cloned.1.call-update) | async-done | bytes 16777232
  1033.1 66.6 %all-reduce.5.cloned.1.call-done = f32[1,128,128]{2,1,0:T(8,128)} async-done(((f32[1,128,128]{2,1,0:T(8,128)}), f32[1,128,128]{2,1,0:T(8,128)}) %all-reduce.5.cloned.1.call-update) | async-done | bytes 65552 | tf_op jit(solution)/shard_map/psum | solution.py:18
  1099.9 52.0 %all-gather.2.cloned.1.call-done = f32[16,128,128]{2,1,0:T(8,128)} async-done(((f32[1,128,128]{2,1,0:T(8,128)}), f32[16,128,128]{2,1,0:T(8,128)}) %all-gather.2.cloned.1.call-update) | async-done | bytes 1048592 | tf_op jit(solution)/shard_map/all_gather | solution.py:175
  1153.8 11.7 cholesky.18
  1166.9 9.8 custom-call.6
  (281 shorter events, 107.1 us)
Async XLA Ops:
  6.5 1024.2 %all-reduce.7.cloned.1.call-start = ((), (), s32[]{:S(2)}) async-start(), calls=%async_computation.2 | async-start | bytes 33554432
  12.4 185.4 %copy-start.4 = (f32[1,9,16]{1,2,0:T(8,128)}, f32[1,9,16]{1,2,0:T(8,128)S(1)}, u32[]{:S(2)}) copy-start(f32[1,9,16]{1,2,0:T(8,128)S(1)} %copy.103) | copy-start | bytes 1732
  12.6 185.2 %copy-start.5 = (f32[1,9,16]{1,2,0:T(8,128)}, f32[1,9,16]{1,2,0:T(8,128)S(1)}, u32[]{:S(2)}) copy-start(f32[1,9,16]{1,2,0:T(8,128)S(1)} %copy.102) | copy-start | bytes 1732
  196.6 184.8 %copy-start.3 = (s32[16,9]{1,0:T(8,128)S(1)}, s32[16,9]{1,0:T(8,128)}, u32[]{:S(2)}) copy-start(s32[16,9]{1,0:T(8,128)} %param.7) | copy-start | bytes 1732
  197.8 368.3 %copy-start.1 = (f32[9,9,1]{1,0,2:T(8,128)S(1)}, f32[9,9,1]{1,0,2:T(8,128)}, u32[]{:S(2)}) copy-start(f32[9,9,1]{1,0,2:T(8,128)} %constant.314) | copy-start | bytes 976
  197.8 368.3 %copy-start.2 = (f32[9,9,16]{2,1,0:T(8,128)S(1)}, f32[9,9,16]{2,1,0:T(8,128)}, u32[]{:S(2)}) copy-start(f32[9,9,16]{2,1,0:T(8,128)} %param.8) | copy-start | bytes 15556
  568.2 174.9 %copy-start.9 = (s32[2]{0:T(128)S(1)}, s32[2]{0:T(128)}, u32[]{:S(2)}) copy-start(s32[2]{0:T(128)} %constant.303) | copy-start | bytes 28
  568.2 175.1 %copy-start.8 = (s32[2]{0:T(128)S(1)}, s32[2]{0:T(128)}, u32[]{:S(2)}) copy-start(s32[2]{0:T(128)} %constant.306) | copy-start | bytes 28
  755.8 1.2 copy-start.6
  755.9 1.8 copy-start
  762.6 1.6 copy-start.7
  820.5 279.2 %all-reduce.5.cloned.1.call-start = ((), (), s32[]{:S(2)}) async-start(), calls=%async_computation | async-start | bytes 131072 | tf_op jit(solution)/shard_map/psum | solution.py:18
  1032.8 119.1 %all-gather.2.cloned.1.call-start = ((), (), s32[]{:S(2)}) async-start(), calls=%async_computation.1 | async-start | bytes 1114112 | tf_op jit(solution)/shard_map/all_gather | solution.py:175
  1153.7 23.0 %slice-start = ((f32[16,128,128]{2,1,0:T(8,128)}), f32[15,128,128]{2,1,0:T(8,128)S(1)}, s32[]{:S(2)}) async-start(f32[16,128,128]{2,1,0:T(8,128)} %all-gather.2.cloned.1.call-done), calls=%async_computation.3 | async-start | bytes 1966080 | tf_op jit(solution)/shard_map/slice | solution.py:180
Sparse Core Ops, SparseCore 0:
  820.6 210.1 all-reduce.6
  1033.4 66.3 all-reduce.4
  1102.2 49.6 all-gather.1
where the time goes:
time: 1190 us
  blocking collectives  551 us (46%)
  waiting for transfers between devices  329 us (28%)
  local copies, waits for them, and re-layouts  120 us (10%)
  other arithmetic  99.5 us (8%)
  matrix products  70.7 us (6%)
  between operations  13.4 us (1%)
    unnamed x4, waiting for transfers between devices  210 us
    all_gather x1, blocking collectives, shards(): lax.all_gather(links_flat, ('blk', 'grid'), axis=1, tiled=True)  185 us
    all_gather x1, blocking collectives, shards(): lax.all_gather(points_flat, ('blk', 'grid'), axis=1, tiled=True)  183 us
    all_gather x1, blocking collectives, shards(): lax.all_gather(extract_flat, ('blk', 'grid'), axis=1, tiled=True)  183 us
    psum x1, waiting for transfers between devices, spread(): return lax.psum(jnp.where(mine, array, jnp.zeros_like(array)), axis)  66.6 us
    all_gather x1, waiting for transfers between devices, shards(): panel_tiles = lax.all_gather(mine, 'grid', axis=0, tiled=True)  52 us
    dot_general x16, matrix products, step(): jnp.dot(kernel_block, trial_phi, precision=lax.Precision.HIGHEST, preferr...  38.3 us
    dynamic_update_slice x16, local copies, waits for them, and re-layouts, step(): lax.dynamic_update_slice_in_dim(potential_wide, current + block, offset, 1)  27.4 us
  transfers between devices with their start and end apart: 3, of which 3 were waited for; matrix products, arithmetic and copies ran while one was open for 0% of the time, Pallas kernels for 0%

commit v1 on v0

--- a/solution.py
+++ b/solution.py
@@ -15,7 +15,7 @@
 
 def spread(array, axis, root):
     mine = lax.axis_index(axis) == root
-    return lax.psum(jnp.where(mine, array, jnp.zeros_like(array)), axis)
+    return jnp.sum(lax.all_gather(jnp.where(mine, array, jnp.zeros_like(array)), axis), axis=0)
 
 
 def bernstein_table():

time: 1190 us -> 1140 us (0.958)
  waiting for transfers between devices: 329 us -> 258 us
  blocking collectives: 551 us -> 574 us
    psum x1 -> x0, waiting for transfers between devices: 66.6 us -> none  [spread(): return lax.psum(jnp.where(mine, array, jnp.zeros_like(array)), axis)]
    all_gather x0 -> x1, blocking collectives: none -> 23.3 us  [spread(): lax.all_gather(jnp.where(mine, array, jnp.zeros_like(array)), axis)]
    unnamed x4 -> x3, waiting for transfers between devices: 210 us -> 210 us
  transfers between devices with their start and end apart: 3 -> 2, of which waited for: 3 -> 2; matrix products, arithmetic and copies ran while one was open for 0% -> 0% of each run, Pallas kernels for 0% -> 0%
where the time goes in v1:
time: 1140 us
  blocking collectives  574 us (50%)
  waiting for transfers between devices  258 us (23%)
  local copies, waits for them, and re-layouts  120 us (11%)
  other arithmetic  99.2 us (9%)
  matrix products  71.4 us (6%)
  between operations  13.7 us (1%)
    unnamed x3, waiting for transfers between devices  210 us
    all_gather x1, blocking collectives, shards(): lax.all_gather(links_flat, ('blk', 'grid'), axis=1, tiled=True)  185 us
    all_gather x1, blocking collectives, shards(): lax.all_gather(points_flat, ('blk', 'grid'), axis=1, tiled=True)  183 us
    all_gather x1, blocking collectives, shards(): lax.all_gather(extract_flat, ('blk', 'grid'), axis=1, tiled=True)  183 us
    all_gather x1, waiting for transfers between devices, shards(): panel_tiles = lax.all_gather(mine, 'grid', axis=0, tiled=True)  47.8 us
    dot_general x16, matrix products, step(): jnp.dot(kernel_block, trial_phi, precision=lax.Precision.HIGHEST, preferr...  38.3 us
    dynamic_update_slice x16, local copies, waits for them, and re-layouts, step(): lax.dynamic_update_slice_in_dim(potential_wide, current + block, offset, 1)  27.4 us
    dot_general x16, matrix products, step(): jnp.einsum('eka,eaw->ekw', local_values(part_extract), ones, precision=la...  23.8 us
  transfers between devices with their start and end apart: 2, of which 2 were waited for; matrix products, arithmetic and copies ran while one was open for 0% of the time, Pallas kernels for 0%

profile of v1, /device:TPU:1, one launch (start us, length us, event | category | flops | bytes accessed | tf_op | source)
XLA Modules:
  0.0 1139.1 jit_solution(16383727444109570755)
XLA Ops:
  13.7 182.9 %all_gather.17 = f32[81,2048]{0,1:T(8,128)S(1)} all-gather(f32[81,16]{0,1:T(8,128)S(1)} %copy.84), channel_id=1, replica_groups=mesh['blk'=8,'grid'=16] {'blk','grid'}, dimensions={1}, use_global_device_ids=true | all-gather | bytes 668736 | tf_op jit(solution)/shard_map/all_gather | solution.py:146
  197.9 183.5 %all_gather.16 = f32[27,2048]{0,1:T(8,128)} all-gather(f32[27,16]{0,1:T(8,128)S(1)} %reshape.427), channel_id=1, replica_groups=mesh['blk'=8,'grid'=16] {'blk','grid'}, dimensions={1}, use_global_device_ids=true | all-gather | bytes 222912 | tf_op jit(solution)/shard_map/all_gather | solution.py:145
  381.4 184.8 %all_gather.18 = s32[9,2048]{0,1:T(8,128)} all-gather(s32[9,16]{0,1:T(8,128)S(1)} %bitcast.102), channel_id=1, replica_groups=mesh['blk'=8,'grid'=16] {'blk','grid'}, dimensions={1}, use_global_device_ids=true | all-gather | bytes 74304 | tf_op jit(solution)/shard_map/all_gather | solution.py:147
  568.2 172.8 %while.20 = (s32[]{:T(128)}, f32[144,2304]{1,0:T(8,128)}, f32[144]{0:T(256)S(1)}, f32[27,2048]{0,1:T(8,128)}, f32[16,9]{1,0:T(8,128)}, /*index=5*/f32[16,9]{1,0:...) while((s32[]{:T(128)}, f32[144,2304]{1,0:T(8,128)}, ...), condition=%wide.wide.region_2.3_spmd.clone.clone, body=%wide.wide.region_0.2_spmd.sunk.clone.clone.sunk | while | flops 548399360 | bytes 5783860 | solution.py:119
  570.6 1.5 fusion.61
  574.0 2.4 convolution_add_fusion.3
  576.4 1.7 dynamic_update_slice.15
  581.4 1.5 fusion.61
  584.8 2.4 convolution_add_fusion.3
  587.2 1.7 dynamic_update_slice.15
  592.3 1.5 fusion.61
  595.7 2.4 convolution_add_fusion.3
  598.1 1.7 dynamic_update_slice.15
  603.1 1.5 fusion.61
  606.5 2.4 convolution_add_fusion.3
  608.9 1.7 dynamic_update_slice.15
  613.9 1.5 fusion.61
  617.3 2.4 convolution_add_fusion.3
  619.7 1.7 dynamic_update_slice.15
  624.6 1.5 fusion.61
  628.0 2.4 convolution_add_fusion.3
  630.4 1.7 dynamic_update_slice.15
  638.8 2.4 convolution_add_fusion.3
  641.2 1.7 dynamic_update_slice.15
  646.2 1.5 fusion.61
  649.6 2.4 convolution_add_fusion.3
  652.0 1.7 dynamic_update_slice.15
  657.1 1.5 fusion.61
  660.5 2.4 convolution_add_fusion.3
  662.9 1.7 dynamic_update_slice.15
  667.9 1.5 fusion.61
  671.3 2.4 convolution_add_fusion.3
  673.7 1.7 dynamic_update_slice.15
  678.7 1.5 fusion.61
  682.1 2.4 convolution_add_fusion.3
  684.5 1.7 dynamic_update_slice.15
  692.9 2.4 convolution_add_fusion.3
  695.3 1.7 dynamic_update_slice.15
  700.3 1.5 fusion.61
  703.7 2.4 convolution_add_fusion.3
  706.1 1.7 dynamic_update_slice.15
  711.1 1.5 fusion.61
  714.5 2.4 convolution_add_fusion.3
  716.9 1.7 dynamic_update_slice.15
  721.9 1.5 fusion.61
  725.3 2.4 convolution_add_fusion.3
  727.7 1.7 dynamic_update_slice.15
  732.7 1.5 fusion.61
  736.1 2.4 convolution_add_fusion.3
  738.5 1.7 dynamic_update_slice.15
  745.1 10.7 scatter_custom_fusion.1
  757.6 1.5 subtract_multiply_fusion
  759.3 3.3 fusion.34
  762.6 1.6 reshape.386
  764.3 6.0 broadcast_in_dim.83
  770.3 16.2 %scatter_fusion = f32[8,2048,256]{2,0,1:T(8,128)} fusion(f32[8,2048,256]{2,0,1:T(8,128)} %broadcast_in_dim.83, s32[144]{0:T(256)S(1)} %bitcast.108, f32[144,8,256]{2,1,0:T(8,128)S(1)} %bitcast.94), kind=kCustom, calls=%fused_computation | custom fusion | flops 294912 | bytes 3539520 | tf_op jit(solution)/shard_map/scatter-add | solution.py:167
  786.4 15.8 %copy.95 = f32[8,2048,256]{2,1,0:T(8,128)} copy(f32[8,2048,256]{2,0,1:T(8,128)} %scatter_fusion) | data formatting | bytes 33554432 | tf_op jit(solution)/shard_map/scatter-add | solution.py:167
  802.3 18.2 %reshape.388 = f32[128,32768]{1,0:T(8,128)} reshape(f32[8,2048,256]{2,1,0:T(8,128)} %copy.95) | data formatting | bytes 33554432 | tf_op jit(solution)/shard_map/reshape | solution.py:169
  820.6 210.2 %all-reduce.4.cloned.1.call-done = f32[128,32768]{1,0:T(8,128)} async-done(((f32[128,32768]{1,0:T(8,128)}), f32[128,32768]{1,0:T(8,128)}) %all-reduce.4.cloned.1.call-update) | async-done | bytes 16777232
  1032.2 23.3 %all-gather = f32[8,128,1,128]{3,1,2,0:T(8,128)S(1)} all-gather(f32[1,128,1,128]{3,1,2,0:T(8,128)S(1)} %broadcast_select_fusion.3), channel_id=2, replica_groups=mesh['blk'=8,'grid'=16] {'blk'}, dimensions={0}, use_global_device_ids=true | all-gather | bytes 589824 | tf_op jit(solution)/shard_map/all_gather | solution.py:18
  1056.7 47.8 %all-gather.4.cloned.1.call-done = f32[2048,128]{0,1:T(8,128)} async-done(((f32[128,128]{0,1:T(8,128)}), f32[2048,128]{0,1:T(8,128)}) %all-gather.4.cloned.1.call-update) | async-done | bytes 1048592 | tf_op jit(solution)/shard_map/all_gather | solution.py:175
  1106.5 11.7 %cholesky.18 = f32[128,128]{1,0:T(8,128)S(1)} custom-call(f32[128,128]{1,0:T(8,128)S(1)} %fusion.23), custom_call_target="Cholesky" | custom-call | tf_op jit(solution)/shard_map/jit(cholesky)/cholesky | solution.py:178
  1119.6 9.8 custom-call.6
  1129.4 1.7 fusion.15
  (282 shorter events, 108.0 us)
Async XLA Ops:
  6.5 1024.2 %all-reduce.4.cloned.1.call-start = ((), (), s32[]{:S(2)}) async-start(), calls=%async_computation.1 | async-start | bytes 33554432
  12.4 185.4 %copy-start.5 = (f32[1,9,16]{1,2,0:T(8,128)}, f32[1,9,16]{1,2,0:T(8,128)S(1)}, u32[]{:S(2)}) copy-start(f32[1,9,16]{1,2,0:T(8,128)S(1)} %copy.107) | copy-start | bytes 1732
  12.6 185.2 %copy-start.6 = (f32[1,9,16]{1,2,0:T(8,128)}, f32[1,9,16]{1,2,0:T(8,128)S(1)}, u32[]{:S(2)}) copy-start(f32[1,9,16]{1,2,0:T(8,128)S(1)} %copy.106) | copy-start | bytes 1732
  196.6 184.8 %copy-start.4 = (s32[16,9]{1,0:T(8,128)S(1)}, s32[16,9]{1,0:T(8,128)}, u32[]{:S(2)}) copy-start(s32[16,9]{1,0:T(8,128)} %param.7) | copy-start | bytes 1732
  197.8 368.3 %copy-start.2 = (f32[9,9,1]{1,0,2:T(8,128)S(1)}, f32[9,9,1]{1,0,2:T(8,128)}, u32[]{:S(2)}) copy-start(f32[9,9,1]{1,0,2:T(8,128)} %constant.314) | copy-start | bytes 976
  197.8 368.3 %copy-start.3 = (f32[9,9,16]{2,1,0:T(8,128)S(1)}, f32[9,9,16]{2,1,0:T(8,128)}, u32[]{:S(2)}) copy-start(f32[9,9,16]{2,1,0:T(8,128)} %param.8) | copy-start | bytes 15556
  568.2 174.9 %copy-start.10 = (s32[2]{0:T(128)S(1)}, s32[2]{0:T(128)}, u32[]{:S(2)}) copy-start(s32[2]{0:T(128)} %constant.303) | copy-start | bytes 28
  568.2 175.1 %copy-start.9 = (s32[2]{0:T(128)S(1)}, s32[2]{0:T(128)}, u32[]{:S(2)}) copy-start(s32[2]{0:T(128)} %constant.306) | copy-start | bytes 28
  755.8 1.2 copy-start.7
  755.9 1.8 copy-start
  762.6 1.6 copy-start.8
  820.5 284.0 %all-gather.4.cloned.1.call-start = ((), (), s32[]{:S(2)}) async-start(), calls=%async_computation | async-start | bytes 1114112 | tf_op jit(solution)/shard_map/all_gather | solution.py:175
  1104.5 24.9 %copy-start.1 = (f32[2048,128]{0,1:T(8,128)S(1)}, f32[2048,128]{0,1:T(8,128)}, u32[]{:S(2)}) copy-start(f32[2048,128]{0,1:T(8,128)} %all-gather.4.cloned.1.call-done) | copy-start | bytes 3145732
Sparse Core Ops, SparseCore 0:
  820.6 210.1 all-reduce.3
  1056.7 47.7 all-gather.3
